TPU v7x, 128 devices: a whole 4x4x4 slice. The times are simulated.
128 devices in a mesh: mem: 8 (over z, y_lo), lev: 16 (over y_hi, x, core).
Axes of the slice: x: 4, y: 4 (y_hi: 2, y_lo: 2; y = y_hi * 2 + y_lo), z: 4, core: 2. Of those that a mesh axis runs over, the one named last changes fastest.
Arguments:
- control: float32 [8, 64, 200, 400], P('mem', 'lev'), may hold values from -6 to 6
- perturbations: bfloat16 [8, 2, 2, 64, 80000], P('mem', None, None, None, 'lev'), may hold values from -4 to 4
- member_scales: float32 [8], P('mem'), may hold values from 0.05 to 0.2
- vertical_loc: float32 [64, 64], replicated, may hold values from -0.75 to 0.75
- latitude_loc: float32 [200, 200], replicated, may hold values from -0.4375 to 0.4375
- longitude_loc: float32 [400, 400], replicated, may hold values from -0.3125 to 0.3125
- observed_index: int32 [2, 65536], P(None, 'lev'), may hold values from 0 to 639999
- observed_weight: float32 [2, 65536], P(None, 'lev'), may hold values from 0.5 to 8
Outputs:
- hessian_vector: float32 [8, 64, 200, 400], P('mem', 'lev')
All inputs are finite; a program needn't handle non-finite values.
Results may differ from a plain program's by a relative error of at most 0.0003.
Values sent between devices are 32-bit elements; how exact they have to be, the bound alone decides.
No kernel may reach another device: no remote copies, remote signals or barrier semaphores. Data moves between devices by JAX's collectives and lax.ppermute only.
A program may use at most 192 MiB of HBM per device.

v0:
```python
import jax
import jax.numpy as jnp
from jax import lax
from jax.sharding import PartitionSpec as P

HIGH = lax.Precision.HIGHEST


def body(
    control,
    perturbations,
    member_scales,
    vertical_loc,
    latitude_loc,
    longitude_loc,
    observed_index,
    observed_weight,
):
    members, level_count, lat_size, lon_size = control.shape
    rows = jnp.einsum("ab,mlbq->mlaq", latitude_loc, control, precision=HIGH)
    horizontal = jnp.einsum("mlaq,oq->mlao", rows, longitude_loc, precision=HIGH)
    flat_fields = horizontal.reshape(members, level_count, lat_size * lon_size)
    columns = lax.all_to_all(flat_fields, "lev", split_axis=2, concat_axis=1, tiled=True)
    localized = jnp.einsum("lk,mkp->mlp", vertical_loc, columns, precision=HIGH)
    scaled = localized * member_scales[:, None, None]
    slot_count, var_count = (perturbations.shape[1], perturbations.shape[2])
    all_levels, column_width = (perturbations.shape[3], perturbations.shape[4])
    span = all_levels * column_width
    slot_rows = jnp.arange(slot_count, dtype=jnp.int32)[:, None]
    partial_value = perturbations[0].astype(jnp.float32) * scaled[0][None, None]
    obs_grid = jnp.zeros((slot_count, var_count * span), jnp.float32)
    obs_grid = obs_grid.at[slot_rows, observed_index].add(observed_weight)
    obs_grid = obs_grid.reshape(slot_count, var_count, all_levels, column_width)
    increment = lax.psum(partial_value, "mem")
    innovation_adj = obs_grid * increment
    summed = jnp.sum(perturbations[0].astype(jnp.float32) * innovation_adj, axis=(0, 1))
    adjoint_list = [summed * member_scales[0]]
    member_adj = jnp.stack(adjoint_list, axis=0)
    vertical_adj = jnp.einsum("kl,mkp->mlp", vertical_loc, member_adj, precision=HIGH)
    level_fields = lax.all_to_all(vertical_adj, "lev", split_axis=1, concat_axis=2, tiled=True)
    level_fields = level_fields.reshape(members, level_count, lat_size, lon_size)
    back_rows = jnp.einsum("ba,mlbq->mlaq", latitude_loc, level_fields, precision=HIGH)
    return control + jnp.einsum("mlaq,qo->mlao", back_rows, longitude_loc, precision=HIGH)


def solution(mesh):
    placed = (
        P("mem", "lev", None, None),
        P("mem", None, None, None, "lev"),
        P("mem"),
        P(),
        P(),
        P(),
        P(None, "lev"),
        P(None, "lev"),
    )
    return jax.shard_map(
        body, mesh=mesh, in_specs=placed, out_specs=P("mem", "lev", None, None), check_vma=False
    )
```

profile of v0, /device:TPU:1, one launch (start us, length us, event | category | flops | bytes accessed | tf_op | source)
XLA Modules:
  0.0 873.8 jit_solution(12977082701842625879)
XLA Ops:
  6.5 0.0 copy-start
  6.5 4.9 fusion.8
  11.4 0.0 copy-done
  11.4 6.5 fusion.6
  17.9 23.7 %copy.36 = f32[4,200,400]{0,2,1:T(8,128)} copy(f32[4,200,400]{2,1,0:T(8,128)S(1)} %fusion.6) | data formatting | bytes 2560000 | tf_op jit(solution)/shard_map/reshape | solution.py:22
  41.6 0.6 broadcast.25
  42.2 371.8 %reduce.4 = f32[80000,4]{1,0:T(8,128)} reduce(f32[80000,1,4]{2,1,0:T(1,128)} %bitcast.71, f32[]{:T(128)} %broadcast.25), dimensions={1}, to_apply=%bitcast.61.reduce_sub_computation | reduce | bytes 2560004
  414.0 37.7 %reshape.67 = f32[16,1,20000]{2,1,0:T(1,128)} reshape(f32[80000,4]{1,0:T(8,128)} %reduce.4) | data formatting | bytes 2560000
  451.6 8.4 all-to-all-start
  460.1 0.2 all-reduce.2.cloned.1.call-start
  460.9 18.9 %all-to-all-done = f32[16,1,20000]{2,1,0:T(1,128)S(1)} async-done(((f32[16,1,20000]{2,1,0:T(1,128)}), f32[16,1,20000]{2,1,0:T(1,128)S(1)}, u32[]{:S(2)}, u32[]{:S(2)}) %all-to-all-start) | async-done | bytes 1280032 | tf_op jit(solution)/shard_map/all_to_all | solution.py:23
  479.9 3.7 reduce.5
  483.6 85.7 %reshape.68 = f32[80000,1,4]{2,1,0:T(1,128)} reshape(f32[16,20000]{1,0:T(8,128)S(1)} %reduce.5) | data formatting | bytes 2560000
  569.3 21.9 %copy.37 = f32[1,4,16,5000]{3,2,1,0:T(8,128)S(1)} copy(f32[1,4,16,5000]{1,3,2,0:T(8,128)} %bitcast.70) | data formatting | bytes 2560000 | tf_op jit(solution)/shard_map/all_to_all | solution.py:23
  591.2 0.8 copy.27
  592.0 0.0 copy-start.4
  592.0 1.5 reshape.48
  593.6 0.0 copy-start.1
  593.6 0.0 copy-done.4
  593.6 2.8 fusion
  596.3 0.0 copy-done.1
  596.3 3.0 convert_multiply_fusion.1
  599.3 0.0 copy-start.5
  599.3 0.0 copy-start.8
  599.3 0.0 copy-start.7
  599.3 0.0 copy-start.6
  599.3 0.0 all-reduce.2.cloned.1.call-update
  599.4 0.7 copy-done.5
  600.1 0.0 copy-done.8
  600.1 0.1 multiply_reduce_fusion
  600.2 0.0 copy-done.7
  600.2 0.1 and_reduce_fusion
  600.4 0.0 copy-done.6
  600.4 0.6 copy.39
  601.1 45.9 %scatter_custom_fusion = f32[1280000]{0:T(1024)} fusion(s32[8192]{0:T(1024)S(1)} %bitcast.76, f32[8192]{0:T(1024)} %bitcast.77, f32[]{:T(128)} %constant.3.clone.1), kind=kCustom, calls=%fused_computation.7 | custom fusion | flops 8192 | bytes 5120512
  646.9 7.2 reshape.44
  654.2 164.8 %all-reduce.2.cloned.1.call-done = f32[2,2,64,5000]{3,2,1,0:T(8,128)} async-done(((f32[2,2,64,5000]{3,2,1,0:T(8,128)}), f32[2,2,64,5000]{3,2,1,0:T(8,128)}) %all-reduce.2.cloned.1.call-update) | async-done | bytes 5120016 | tf_op jit(solution)/shard_map/psum | solution.py:34
  819.0 5.5 fusion.1
  824.5 1.4 convolution_bitcast_fusion
  825.9 1.3 copy.28
  827.2 27.5 %all_to_all.30 = f32[1,64,5000]{2,0,1:T(1,128)S(1)} all-to-all(f32[1,64,5000]{2,0,1:T(1,128)S(1)} %copy.28), channel_id=1, replica_groups=mesh['mem'=8,'lev'=16] {'lev'}, dimensions={1} | all-to-all | bytes 2560000 | tf_op jit(solution)/shard_map/all_to_all | solution.py:40
  854.7 1.8 copy.41
  856.6 0.0 copy-start.3
  856.6 2.0 reshape.49
  858.5 0.0 copy-done.3
  858.6 0.0 copy-start.2
  858.6 3.3 fusion.16
  861.9 0.0 copy-done.2
  861.9 4.8 bitcast_add_fusion
  (4 shorter events, 0.1 us)
Async XLA Ops:
  6.5 4.9 copy-start
  451.6 28.2 %all-to-all-start = ((f32[16,1,20000]{2,1,0:T(1,128)}), f32[16,1,20000]{2,1,0:T(1,128)S(1)}, u32[]{:S(2)}, u32[]{:S(2)}) async-start(f32[16,1,20000]{2,1,0:T(1,128)} %reshape.67), calls=%async_computation | async-start | bytes 2572288 | tf_op jit(solution)/shard_map/all_to_all | solution.py:23
  460.1 358.9 %all-reduce.2.cloned.1.call-start = ((), (), s32[]{:S(2)}) async-start(), calls=%async_computation.2 | async-start | bytes 10485760 | tf_op jit(solution)/shard_map/psum | solution.py:34
  592.0 1.5 copy-start.4
  593.6 2.8 copy-start.1
  599.3 0.8 copy-start.5
  599.3 0.8 copy-start.8
  599.3 0.9 copy-start.7
  599.3 1.1 copy-start.6
  856.6 2.0 copy-start.3
  858.6 3.3 copy-start.2
Sparse Core Ops, SparseCore 0:
  599.5 219.4 all-reduce.1
where the time goes:
time: 881 us; the launch traced here: 874 us
  other arithmetic  430 us (49%)
  local copies, waits for them, and re-layouts  186 us (21%)
  waiting for transfers between devices  184 us (21%)
  blocking collectives  27.5 us (3%)
  matrix products  23.6 us (3%)
  between operations  14.5 us (2%)
    unnamed x5, other arithmetic  418 us
    psum x1, waiting for transfers between devices, body(): increment = lax.psum(partial_value, 'mem')  165 us
    unnamed x23, local copies, waits for them, and re-layouts  125 us
    all_to_all x1, blocking collectives, body(): lax.all_to_all(vertical_adj, 'lev', split_axis=1, concat_axis=2, tiled=True)  27.5 us
    reshape x1, local copies, waits for them, and re-layouts, body(): flat_fields = horizontal.reshape(members, level_count, lat_size * lon_size)  23.7 us
    all_to_all x2, local copies, waits for them, and re-layouts, body(): lax.all_to_all(flat_fields, 'lev', split_axis=2, concat_axis=1, tiled=True)  22.7 us
    all_to_all x1, waiting for transfers between devices, body(): lax.all_to_all(flat_fields, 'lev', split_axis=2, concat_axis=1, tiled=True)  18.9 us
  transfers between devices with their start and end apart: 2, of which 2 were waited for; matrix products, arithmetic and copies ran while one was open for 6% of the time, Pallas kernels for 0%

commit v1 on v0

--- a/solution.py
+++ b/solution.py
@@ -16,11 +16,20 @@
     observed_index,
     observed_weight,
 ):
+
+    def sheets_form(matrix, row_axis):
+        return jnp.concatenate(
+            lax.all_to_all(
+                jnp.stack(jnp.split(matrix, lax.axis_size(row_axis), axis=2)), row_axis, 0, 0
+            ),
+            axis=1,
+        )
+
     members, level_count, lat_size, lon_size = control.shape
     rows = jnp.einsum("ab,mlbq->mlaq", latitude_loc, control, precision=HIGH)
     horizontal = jnp.einsum("mlaq,oq->mlao", rows, longitude_loc, precision=HIGH)
     flat_fields = horizontal.reshape(members, level_count, lat_size * lon_size)
-    columns = lax.all_to_all(flat_fields, "lev", split_axis=2, concat_axis=1, tiled=True)
+    columns = sheets_form(flat_fields, "lev")
     localized = jnp.einsum("lk,mkp->mlp", vertical_loc, columns, precision=HIGH)
     scaled = localized * member_scales[:, None, None]
     slot_count, var_count = (perturbations.shape[1], perturbations.shape[2])

time: 881 us -> 350 us (0.40)
  other arithmetic: 430 us -> 54.6 us
  local copies, waits for them, and re-layouts: 186 us -> 36.6 us
    unnamed x5 -> x4, other arithmetic: 418 us -> 46.1 us
    unnamed x23 -> x37, local copies, waits for them, and re-layouts: 125 us -> 19.7 us
    all_to_all x2 -> x0, local copies, waits for them, and re-layouts: 22.7 us -> none  [body(): lax.all_to_all(flat_fields, 'lev', split_axis=2, concat_axis=1, tiled=True)]
    reshape x1, local copies, waits for them, and re-layouts: 23.7 us -> 2.43 us  [body(): flat_fields = horizontal.reshape(members, level_count, lat_size * lon_size)]
  transfers between devices with their start and end apart: 2 -> 2, of which waited for: 2 -> 2; matrix products, arithmetic and copies ran while one was open for 6% -> 15% of each run, Pallas kernels for 0% -> 0%
where the time goes in v1:
time: 350 us; the launch traced here: 349 us
  waiting for transfers between devices  184 us (53%)
  other arithmetic  54.6 us (16%)
  local copies, waits for them, and re-layouts  36.6 us (10%)
  blocking collectives  27.3 us (8%)
  matrix products  23.6 us (7%)
  between operations  14.2 us (4%)
  starting transfers between devices  8.65 us (2%)
    psum x1, waiting for transfers between devices, body(): increment = lax.psum(partial_value, 'mem')  165 us
    unnamed x4, other arithmetic  46.1 us
    all_to_all x1, blocking collectives, body(): lax.all_to_all(vertical_adj, 'lev', split_axis=1, concat_axis=2, tiled=True)  27.3 us
    unnamed x37, local copies, waits for them, and re-layouts  19.7 us
    all_to_all x1, waiting for transfers between devices, sheets_form(): lax.all_to_all(jnp.stack(jnp.split(matrix, lax.axis_size(row_axis), axis=...  19.2 us
    all_to_all x1, starting transfers between devices, sheets_form(): lax.all_to_all(jnp.stack(jnp.split(matrix, lax.axis_size(row_axis), axis=...  8.43 us
    reshape x1, local copies, waits for them, and re-layouts, body(): obs_grid = obs_grid.reshape(slot_count, var_count, all_levels, column_width)  7.09 us
  transfers between devices with their start and end apart: 2, of which 2 were waited for; matrix products, arithmetic and copies ran while one was open for 15% of the time, Pallas kernels for 0%

profile of v1, /device:TPU:1, one launch (start us, length us, event | category | flops | bytes accessed | tf_op | source)
XLA Modules:
  0.0 349.2 jit_solution(3177430189921122589)
XLA Ops:
  6.5 0.0 copy-start
  6.5 4.9 %fusion.8 = f32[4,400,200]{2,1,0:T(8,128)S(1)} fusion(f32[1,4,200,400]{3,2,1,0:T(8,128)} %param.8, f32[200,200]{1,0:T(8,128)} %param.12), kind=kOutput, calls=%fused_computation.14 | convolution fusion | flops 768000000 | bytes 2720000 | tf_op jit(solution)/shard_map/ab,mlbq->mlaq/dot_general | solution.py:29
  11.4 0.0 copy-done
  11.4 6.5 %fusion.6 = f32[4,200,400]{2,1,0:T(8,128)S(1)} fusion(f32[4,400,200]{2,1,0:T(8,128)S(1)} %fusion.8, f32[400,400]{1,0:T(8,128)S(1)} %copy-done), kind=kOutput, calls=%fused_computation.11 | convolution fusion | flops 1536000000 | bytes 3200000 | tf_op jit(solution)/shard_map/mlaq,oq->mlao/dot_general | solution.py:30
  17.9 2.4 reshape.48
  20.3 0.0 copy-start.3
  20.3 1.6 fusion.34
  22.0 1.6 fusion.33
  23.6 1.6 fusion.32
  25.2 1.6 fusion.31
  26.9 1.6 fusion.30
  28.5 1.6 fusion.29
  30.1 1.6 fusion.28
  31.8 1.6 fusion.27
  33.4 0.0 copy-done.3
  33.4 0.7 fusion.26
  34.1 0.7 fusion.25
  34.9 0.7 fusion.24
  35.6 0.7 fusion.23
  36.4 0.7 fusion.22
  37.1 0.7 fusion.21
  37.9 0.7 fusion.20
  38.6 0.7 fusion.19
  39.4 8.4 %all-to-all-start = ((f32[16,1,4,5000]{3,2,1,0:T(4,128)}), f32[16,1,4,5000]{3,2,1,0:T(4,128)S(1)}, u32[]{:S(2)}, u32[]{:S(2)}) async-start(f32[16,1,4,5000]{3,2,1,0:T(4,128)} %fusion.19), calls=%async_computation | async-start | bytes 2621440 | tf_op jit(solution)/shard_map/all_to_all | solution.py:22
  47.8 0.2 all-reduce.2.cloned.1.call-start
  48.7 0.0 copy-start.5
  48.7 19.2 %all-to-all-done = f32[16,1,4,5000]{3,2,1,0:T(4,128)S(1)} async-done(((f32[16,1,4,5000]{3,2,1,0:T(4,128)}), f32[16,1,4,5000]{3,2,1,0:T(4,128)S(1)}, u32[]{:S(2)}, u32[]{:S(2)}) %all-to-all-start) | async-done | bytes 1280032 | tf_op jit(solution)/shard_map/all_to_all | solution.py:22
  67.9 1.5 reshape.49
  69.4 0.0 copy-done.5
  69.4 0.0 copy-start.1
  69.4 2.8 fusion
  72.2 0.0 copy-done.1
  72.2 3.0 convert_multiply_fusion.1
  75.1 0.0 copy-start.6
  75.1 0.0 copy-start.8
  75.1 0.0 copy-start.9
  75.1 0.0 copy-start.7
  75.1 0.0 all-reduce.2.cloned.1.call-update
  75.2 0.7 copy-done.6
  75.9 0.0 copy-done.8
  75.9 0.1 multiply_reduce_fusion
  76.0 0.0 copy-done.9
  76.0 0.1 and_reduce_fusion
  76.2 0.0 copy-done.7
  76.2 0.6 copy.28
  76.9 45.9 %scatter_custom_fusion = f32[1280000]{0:T(1024)} fusion(s32[8192]{0:T(1024)S(1)} %bitcast.132, f32[8192]{0:T(1024)} %bitcast.133, f32[]{:T(128)} %constant.3.clone.1), kind=kCustom, calls=%fused_computation.7 | custom fusion | flops 8192 | bytes 5120512
  122.7 7.1 %reshape.45 = f32[2,2,64,5000]{3,2,1,0:T(8,128)} reshape(f32[1280000]{0:T(1024)} %scatter_custom_fusion) | data formatting | bytes 10240000 | tf_op jit(solution)/shard_map/reshape | solution.py:42
  129.8 165.0 %all-reduce.2.cloned.1.call-done = f32[2,2,64,5000]{3,2,1,0:T(8,128)} async-done(((f32[2,2,64,5000]{3,2,1,0:T(8,128)}), f32[2,2,64,5000]{3,2,1,0:T(8,128)}) %all-reduce.2.cloned.1.call-update) | async-done | bytes 5120016 | tf_op jit(solution)/shard_map/psum | solution.py:43
  294.8 5.5 %fusion.1 = f32[64,5000]{1,0:T(8,128)S(1)} fusion(f32[2,2,64,5000]{3,2,1,0:T(8,128)} %reshape.45, f32[2,2,64,5000]{3,2,1,0:T(8,128)} %all-reduce.2.cloned.1.call-done, bf16[1,2,2,64,5000]{4,3,2,1,0:T(8,128)(2,1)S(1)} %copy-done.1), kind=kLoop, calls=%fused_computation.6 | loop fusion | flops 4800000 | bytes 14080000 | tf_op jit(solution)/shard_map/reduce_sum | solution.py:45
  300.3 1.4 convolution_bitcast_fusion
  301.7 1.3 copy.19
  303.1 27.3 %all_to_all.20 = f32[1,64,5000]{2,0,1:T(1,128)S(1)} all-to-all(f32[1,64,5000]{2,0,1:T(1,128)S(1)} %copy.19), channel_id=1, replica_groups=mesh['mem'=8,'lev'=16] {'lev'}, dimensions={1} | all-to-all | bytes 2560000 | tf_op jit(solution)/shard_map/all_to_all | solution.py:49
  330.4 1.8 copy.30
  332.2 0.0 copy-start.4
  332.2 2.0 reshape.50
  334.2 0.0 copy-done.4
  334.2 0.0 copy-start.2
  334.2 3.3 fusion.16
  337.5 0.0 copy-done.2
  337.5 4.8 %bitcast_add_fusion = f32[1,4,200,400]{3,2,1,0:T(8,128)} fusion(f32[1,4,200,400]{3,2,1,0:T(8,128)S(1)} %copy-done.2, f32[4,400,200]{2,1,0:T(8,128)S(1)} %fusion.16, f32[400,400]{1,0:T(8,128)S(1)} %copy-done), kind=kOutput, calls=%fused_computation.13 | convolution fusion | flops 1536320000 | bytes 4480000 | tf_op jit(solution)/shard_map/mlaq,qo->mlao/dot_general | solution.py:52
  (4 shorter events, 0.1 us)
Async XLA Ops:
  6.5 4.9 %copy-start = (f32[400,400]{1,0:T(8,128)S(1)}, f32[400,400]{1,0:T(8,128)}, u32[]{:S(2)}) copy-start(f32[400,400]{1,0:T(8,128)} %param.13) | copy-start | bytes 1920004
  20.3 13.1 %copy-start.3 = (f32[1,4,80000]{2,1,0:T(4,128)S(1)}, f32[1,4,80000]{2,1,0:T(4,128)}, u32[]{:S(2)}) copy-start(f32[1,4,80000]{2,1,0:T(4,128)} %reshape.48) | copy-start | bytes 3840004
  39.4 28.5 %all-to-all-start = ((f32[16,1,4,5000]{3,2,1,0:T(4,128)}), f32[16,1,4,5000]{3,2,1,0:T(4,128)S(1)}, u32[]{:S(2)}, u32[]{:S(2)}) async-start(f32[16,1,4,5000]{3,2,1,0:T(4,128)} %fusion.19), calls=%async_computation | async-start | bytes 2621440 | tf_op jit(solution)/shard_map/all_to_all | solution.py:22
  47.8 247.1 %all-reduce.2.cloned.1.call-start = ((), (), s32[]{:S(2)}) async-start(), calls=%async_computation.2 | async-start | bytes 10485760 | tf_op jit(solution)/shard_map/psum | solution.py:43
  48.7 20.7 %copy-start.5 = (f32[64,64]{1,0:T(8,128)S(1)}, f32[64,64]{1,0:T(8,128)}, u32[]{:S(2)}) copy-start(f32[64,64]{1,0:T(8,128)} %param.11) | copy-start | bytes 49156
  69.4 2.8 copy-start.1
  75.1 0.8 copy-start.6
  75.1 0.8 copy-start.8
  75.1 0.9 copy-start.9
  75.1 1.1 copy-start.7
  332.2 2.0 copy-start.4
  334.2 3.3 copy-start.2
Sparse Core Ops, SparseCore 0:
  75.3 219.5 all-reduce.1

commit v2 on v0

--- a/solution.py
+++ b/solution.py
@@ -31,7 +31,8 @@
     obs_grid = jnp.zeros((slot_count, var_count * span), jnp.float32)
     obs_grid = obs_grid.at[slot_rows, observed_index].add(observed_weight)
     obs_grid = obs_grid.reshape(slot_count, var_count, all_levels, column_width)
-    increment = lax.psum(partial_value, "mem")
+    heard = lax.all_gather(partial_value, axis_name="mem")
+    increment = jnp.sum(heard, 0)
     innovation_adj = obs_grid * increment
     summed = jnp.sum(perturbations[0].astype(jnp.float32) * innovation_adj, axis=(0, 1))
     adjoint_list = [summed * member_scales[0]]

time: 881 us -> 1470 us (1.67)
  waiting for transfers between devices: 184 us -> 759 us
  other arithmetic: 430 us -> 448 us
    all_gather x0 -> x1, waiting for transfers between devices: none -> 740 us  [body(): heard = lax.all_gather(partial_value, axis_name='mem')]
    psum x1 -> x0, waiting for transfers between devices: 165 us -> none  [body(): increment = lax.psum(partial_value, 'mem')]
    reduce_sum x0 -> x1, other arithmetic: none -> 18.1 us  [body(): increment = jnp.sum(heard, 0)]
  transfers between devices with their start and end apart: 2 -> 2, of which waited for: 2 -> 2; matrix products, arithmetic and copies ran while one was open for 6% -> 4% of each run, Pallas kernels for 0% -> 0%
where the time goes in v2:
time: 1470 us
  waiting for transfers between devices  759 us (52%)
  other arithmetic  448 us (30%)
  local copies, waits for them, and re-layouts  186 us (13%)
  blocking collectives  27.2 us (2%)
  matrix products  23.6 us (2%)
    all_gather x1, waiting for transfers between devices, body(): heard = lax.all_gather(partial_value, axis_name='mem')  740 us
    unnamed x5, other arithmetic  418 us
    unnamed x23, local copies, waits for them, and re-layouts  125 us
  transfers between devices with their start and end apart: 2, of which 2 were waited for; matrix products, arithmetic and copies ran while one was open for 4% of the time, Pallas kernels for 0%

profile of v2, /device:TPU:1, one launch (start us, length us, event | category | flops | bytes accessed | tf_op | source)
XLA Modules:
  0.0 1467.1 jit_solution(9299228699560873250)
XLA Ops:
  6.5 0.0 copy-start
  6.5 4.9 fusion.9
  11.4 0.0 copy-done
  11.4 6.5 fusion.7
  17.9 23.7 %copy.36 = f32[4,200,400]{0,2,1:T(8,128)} copy(f32[4,200,400]{2,1,0:T(8,128)S(1)} %fusion.7) | data formatting | bytes 2560000 | tf_op jit(solution)/shard_map/reshape | solution.py:22
  41.6 0.6 broadcast.26
  42.2 371.8 %reduce.4 = f32[80000,4]{1,0:T(8,128)} reduce(f32[80000,1,4]{2,1,0:T(1,128)} %bitcast.73, f32[]{:T(128)} %broadcast.26), dimensions={1}, to_apply=%bitcast.63.reduce_sub_computation | reduce | bytes 2560004
  414.0 37.7 %reshape.67 = f32[16,1,20000]{2,1,0:T(1,128)} reshape(f32[80000,4]{1,0:T(8,128)} %reduce.4) | data formatting | bytes 2560000
  451.6 8.4 all-to-all-start
  460.1 0.2 all-gather.2.cloned.1.call-start
  460.9 18.9 %all-to-all-done = f32[16,1,20000]{2,1,0:T(1,128)S(1)} async-done(((f32[16,1,20000]{2,1,0:T(1,128)}), f32[16,1,20000]{2,1,0:T(1,128)S(1)}, u32[]{:S(2)}, u32[]{:S(2)}) %all-to-all-start) | async-done | bytes 1280032 | tf_op jit(solution)/shard_map/all_to_all | solution.py:23
  479.9 3.7 reduce.5
  483.6 85.7 %reshape.68 = f32[80000,1,4]{2,1,0:T(1,128)} reshape(f32[16,20000]{1,0:T(8,128)S(1)} %reduce.5) | data formatting | bytes 2560000
  569.3 21.9 %copy.37 = f32[1,4,16,5000]{3,2,1,0:T(8,128)S(1)} copy(f32[1,4,16,5000]{1,3,2,0:T(8,128)} %bitcast.72) | data formatting | bytes 2560000 | tf_op jit(solution)/shard_map/all_to_all | solution.py:23
  591.2 0.8 copy.27
  592.0 0.0 copy-start.4
  592.0 1.5 reshape.48
  593.6 0.0 copy-start.1
  593.6 0.0 copy-done.4
  593.6 2.8 fusion
  596.3 0.0 copy-done.1
  596.3 2.9 convert_multiply_fusion
  599.2 0.0 copy-start.5
  599.2 0.0 copy-start.8
  599.2 0.0 copy-start.7
  599.2 0.0 copy-start.6
  599.2 0.0 all-gather.2.cloned.1.call-update
  599.2 0.7 copy-done.5
  600.0 0.0 copy-done.8
  600.0 0.1 multiply_reduce_fusion
  600.1 0.0 copy-done.7
  600.1 0.1 and_reduce_fusion
  600.3 0.0 copy-done.6
  600.3 0.6 copy.39
  601.0 45.9 %scatter_custom_fusion = f32[1280000]{0:T(1024)} fusion(s32[8192]{0:T(1024)S(1)} %bitcast.78, f32[8192]{0:T(1024)} %bitcast.79, f32[]{:T(128)} %constant.3.clone.1), kind=kCustom, calls=%fused_computation.8 | custom fusion | flops 8192 | bytes 5120512
  646.9 7.3 reshape.44
  654.2 740.3 %all-gather.2.cloned.1.call-done = f32[8,2,2,64,5000]{4,3,2,1,0:T(8,128)} async-done(((f32[1,2,2,64,5000]{4,3,2,1,0:T(8,128)}), f32[8,2,2,64,5000]{4,3,2,1,0:T(8,128)}) %all-gather.2.cloned.1.call-update) | async-done | bytes 40960016 | tf_op jit(solution)/shard_map/all_gather | solution.py:34
  1394.5 18.1 %reduce_sum.18 = f32[2,2,64,5000]{3,2,1,0:T(8,128)} reduce(f32[8,2,2,64,5000]{4,3,2,1,0:T(8,128)} %all-gather.2.cloned.1.call-done, f32[]{:T(128)} %constant.3.clone.1), dimensions={0}, to_apply=%region_1.0 | reduce | flops 8960000 | bytes 46080004 | tf_op jit(solution)/shard_map/reduce_sum | solution.py:35
  1412.7 5.5 fusion.2
  1418.2 1.4 convolution_bitcast_fusion
  1419.5 1.3 copy.28
  1420.9 27.2 %all_to_all.30 = f32[1,64,5000]{2,0,1:T(1,128)S(1)} all-to-all(f32[1,64,5000]{2,0,1:T(1,128)S(1)} %copy.28), channel_id=1, replica_groups=mesh['mem'=8,'lev'=16] {'lev'}, dimensions={1} | all-to-all | bytes 2560000 | tf_op jit(solution)/shard_map/all_to_all | solution.py:41
  1448.1 1.8 copy.41
  1449.9 0.0 copy-start.3
  1449.9 2.0 reshape.49
  1451.9 0.0 copy-done.3
  1451.9 0.0 copy-start.2
  1451.9 3.3 fusion.17
  1455.2 0.0 copy-done.2
  1455.2 4.8 bitcast_add_fusion
  (4 shorter events, 0.1 us)
Async XLA Ops:
  6.5 4.9 copy-start
  451.6 28.2 %all-to-all-start = ((f32[16,1,20000]{2,1,0:T(1,128)}), f32[16,1,20000]{2,1,0:T(1,128)S(1)}, u32[]{:S(2)}, u32[]{:S(2)}) async-start(f32[16,1,20000]{2,1,0:T(1,128)} %reshape.67), calls=%async_computation | async-start | bytes 2572288 | tf_op jit(solution)/shard_map/all_to_all | solution.py:23
  460.1 934.5 %all-gather.2.cloned.1.call-start = ((), (), s32[]{:S(2)}) async-start(), calls=%async_computation.2 | async-start | bytes 47185920 | tf_op jit(solution)/shard_map/all_gather | solution.py:34
  592.0 1.5 copy-start.4
  593.6 2.8 copy-start.1
  599.2 0.8 copy-start.5
  599.2 0.8 copy-start.8
  599.2 0.9 copy-start.7
  599.2 1.1 copy-start.6
  1449.9 2.0 copy-start.3
  1451.9 3.3 copy-start.2
Sparse Core Ops, SparseCore 0:
  599.4 795.1 all-gather.1
